TPU v7x, 256 devices: a whole 4x4x8 slice. The times are simulated.
256 devices in a mesh: grp: 16 (over y, x), tp: 16 (over z, core).
Axes of the slice: x: 4, y: 4, z: 8, core: 2. Of those that a mesh axis runs over, the one named last changes fastest.
Arguments:
- hidden: bfloat16 [294912, 5120], P(('grp', 'tp')), may hold values from -6 to 6
- lengths: int32 [16, 16], P('grp'), may hold values from 1 to 1152, 7372 in all within a row
- kv_weight: bfloat16 [5120, 1024], P('grp', 'tp'), may hold values from -0.078125 to 0.078125
- input_gain: float32 [5120], replicated, may hold values from 0.1 to 1.9
- key_gain: float32 [128], replicated, may hold values from 0.1 to 1.9
Outputs:
- cache_pages: bfloat16 [1280, 128, 1024], P(('grp', 'tp'))
Inputs may be any that keep to these rules, and one draw needn't show every extreme that they name: In each group's row the 16 lengths sum to 7372 and the largest equals 1152.
All inputs are finite; a program needn't handle non-finite values.
Results may differ from a plain program's by a relative error of at most 0.0049.
Values may be sent and summed in bfloat16 or wider, within the bound.
A program may use at most 64 MiB of HBM per device.

v0:
```python
import math
import jax
import jax.numpy as jnp
from jax import lax
from jax.sharding import PartitionSpec as P

HD = 128
KVH = 4
BLK = 128
rope_base = 1000000.0
norm_eps = 1e-06


def normalize(token_rows, input_gain):
    values = token_rows.astype(jnp.float32)
    row_scale = lax.rsqrt(jnp.mean(values * values, axis=-1, keepdims=True) + norm_eps)
    return (values * row_scale * input_gain).astype(jnp.bfloat16)


def finish(projected, positions, valid, key_gain):
    key_width = KVH * HD
    half_dim = HD // 2
    row_count = projected.shape[0]
    key_part = projected[:, :key_width].reshape(row_count, KVH, HD)
    key_scale = lax.rsqrt(jnp.mean(key_part * key_part, axis=-1, keepdims=True) + norm_eps)
    key_part = key_part * key_scale * key_gain
    exponent = jnp.arange(half_dim, dtype=jnp.float32) * (2.0 / HD)
    inverse = jnp.exp(exponent * -math.log(rope_base))
    angles = positions.astype(jnp.float32)[:, None] * inverse[None, :]
    cosine = jnp.cos(angles)[:, None, :]
    sine_part = jnp.sin(angles)[:, None, :]
    lower_half = key_part[..., :half_dim]
    upper_half = key_part[..., half_dim:]
    turned = jnp.concatenate(
        [
            lower_half * cosine - upper_half * sine_part,
            upper_half * cosine + lower_half * sine_part,
        ],
        axis=-1,
    )
    merged = jnp.concatenate(
        [turned.reshape(row_count, key_width), projected[:, key_width:]], axis=-1
    )
    return jnp.where(valid[:, None], merged, 0.0).astype(jnp.bfloat16)


def project(normed, kv_weight):
    all_rows = lax.all_gather(kv_weight, "grp", axis=0, tiled=True)
    return jnp.dot(
        normed,
        lax.all_gather(all_rows, "tp", axis=1, tiled=True),
        preferred_element_type=jnp.float32,
    )


def local(hidden, lengths, kv_weight, input_gain, key_gain):
    tp_count = lax.axis_size("tp")
    my_index = lax.axis_index("tp")
    own_blocks = hidden.shape[0] // BLK
    live_tokens = 2 * tp_count * own_blocks * BLK // 5
    page_count = ((live_tokens + BLK - 1) // BLK + 2 * tp_count - 2) // tp_count
    per_peer = (own_blocks + tp_count - 1) // tp_count
    cache_width = 2 * KVH * HD
    group_len = lengths[0]
    block_counts = (group_len + (BLK - 1)) // BLK
    block_ends = jnp.cumsum(block_counts)
    block_starts = block_ends - block_counts
    offsets = jnp.arange(BLK, dtype=jnp.int32)
    my_start = block_starts[my_index]
    my_count = block_counts[my_index]
    my_length = group_len[my_index]
    outbound = (
        jnp.arange(tp_count, dtype=jnp.int32)[:, None] - my_start
    ) % tp_count + tp_count * jnp.arange(per_peer, dtype=jnp.int32)[None, :]
    outbound = outbound.reshape(-1)
    sending = outbound < my_count
    picked_local = jnp.minimum(outbound, own_blocks - 1)
    page_ranks = tp_count * jnp.arange(page_count, dtype=jnp.int32) + my_index
    anchor = jnp.minimum(
        jnp.sum((block_ends[None, :] <= page_ranks[:, None]).astype(jnp.int32), axis=1),
        tp_count - 1,
    )
    block_index = page_ranks - block_starts[anchor]
    page_live = page_ranks < block_ends[-1]
    chosen = anchor * per_peer + jnp.clip(block_index // tp_count, 0, per_peer - 1)
    projected = project(normalize(hidden, input_gain), kv_weight)
    own_pos = (jnp.arange(own_blocks, dtype=jnp.int32)[:, None] * BLK + offsets[None, :]).reshape(
        -1
    )
    own_cache = finish(projected, own_pos, own_pos < my_length, key_gain).reshape(
        own_blocks, BLK, cache_width
    )
    outgoing = jnp.where(
        sending[:, None, None],
        jnp.take(own_cache, picked_local, axis=0),
        jnp.zeros((), jnp.bfloat16),
    )
    arrived = lax.all_to_all(outgoing, "tp", split_axis=0, concat_axis=0, tiled=True)
    cache_pages = jnp.take(arrived, chosen, axis=0)
    return jnp.where(page_live[:, None, None], cache_pages, jnp.zeros((), jnp.bfloat16))


def solution(mesh):
    placed = (P(("grp", "tp"), None), P("grp", None), P("grp", "tp"), P(), P())
    return jax.shard_map(
        local, mesh=mesh, in_specs=placed, out_specs=P(("grp", "tp"), None, None), check_vma=False
    )
```

profile of v0, /device:TPU:1, one launch (start us, length us, event | category | flops | bytes accessed | tf_op | source)
XLA Modules:
  0.0 249.6 jit_solution(15077039572765754980)
XLA Ops:
  6.5 0.0 copy-start.7
  6.5 0.0 all-gather.3.cloned.1.call-start
  6.5 20.4 %all-gather = bf16[16,320,64]{1,2,0:T(8,128)(2,1)S(1)} all-gather(bf16[1,320,64]{1,2,0:T(8,128)(2,1)} %bitcast.44), channel_id=1, replica_groups=mesh['grp'=16,'tp'=16] {'grp'}, dimensions={0}, use_global_device_ids=true | all-gather | bytes 696320 | tf_op jit(solution)/shard_map/all_gather | solution.py:48
  26.9 0.5 copy.17
  27.4 1.5 reshape.400
  28.9 0.0 all-gather.3.cloned.1.call-update
  28.9 0.0 copy-done.7
  28.9 0.6 constant_dynamic-slice_fusion
  29.5 0.1 copy.16
  29.7 0.1 reduce
  29.8 0.0 copy-start.4
  29.8 0.6 dynamic_slice.9
  30.4 0.6 dynamic_slice.10
  31.0 0.6 fusion.13
  31.6 1.8 compare_and_fusion
  33.4 0.6 pad_clamp_fusion.1
  34.0 0.6 fusion.8
  34.6 0.1 convert_bitcast_fusion
  34.7 0.0 copy-done.4
  34.7 0.0 copy-start.8
  34.7 6.7 %fusion = f32[1152]{0:T(1024)S(1)} fusion(bf16[1152,5120]{1,0:T(8,128)(2,1)} %param.5), kind=kLoop, calls=%fused_computation.5 | loop fusion | flops 17693568 | bytes 11801088 | tf_op jit(solution)/shard_map/reduce_sum | solution.py:16
  41.4 3.5 %multiply_cosine_fusion = (f32[1152,64]{1,0:T(8,128)}, f32[1152,64]{1,0:T(8,128)}) fusion(f32[64]{0:T(128)S(1)} %multiply_exponential_fusion, f32[1152]{0:T(1024)S(1)} %convert_bitcast_fusion), kind=kLoop, calls=%fused_computation.21 | loop fusion | flops 73728 | bytes 594688 | tf_op jit(solution)/shard_map/cos | solution.py:30
  44.9 56.4 %all-gather.3.cloned.1.call-done = bf16[5120,1024]{0,1:T(8,128)(2,1)} async-done(((bf16[5120,64]{0,1:T(8,128)(2,1)}), bf16[5120,1024]{0,1:T(8,128)(2,1)}) %all-gather.3.cloned.1.call-update) | async-done | bytes 10485776 | tf_op jit(solution)/shard_map/all_gather | solution.py:51
  101.3 0.0 copy-done.8
  101.3 16.9 %fusion.3 = f32[1152,1024]{1,0:T(8,128)S(1)} fusion(bf16[5120,1024]{0,1:T(8,128)(2,1)} %all-gather.3.cloned.1.call-done, bf16[1152,5120]{1,0:T(8,128)(2,1)} %param.5, f32[5120]{0:T(1024)S(1)} %copy-done.8, f32[1152]{0:T(1024)S(1)} %add_rsqrt_fusion.1), kind=kOutput, calls=%fused_computation.8 | convolution fusion | flops 12103188480 | bytes 27025920 | tf_op jit(solution)/shard_map/dot_general | solution.py:49
  118.2 1.7 slice.28
  119.9 0.2 slice.31
  120.1 2.6 %reshape.374 = f32[1152,4,128]{2,1,0:T(4,128)S(1)} reshape(f32[1152,512]{1,0:T(8,128)} %slice.28) | data formatting | bytes 4718592 | tf_op jit(solution)/shard_map/reshape | solution.py:24
  122.7 0.0 copy-start.6
  122.7 2.0 multiply_reduce_fusion
  124.8 0.1 add_rsqrt_fusion
  124.9 0.0 copy-done.6
  124.9 0.0 copy-start
  124.9 0.0 copy-start.1
  124.9 1.5 multiply_multiply_fusion
  126.4 0.0 copy-done
  126.4 0.0 copy-done.1
  126.4 1.8 multiply_subtract_fusion
  128.3 1.7 pad_maximum_fusion
  129.9 1.3 concatenate.12
  131.2 1.7 fusion.7
  132.9 0.0 copy-start.2
  132.9 0.0 copy-start.3
  132.9 2.9 %gather_fusion.1 = bf16[16,128,1024]{2,1,0:T(8,128)(2,1)} fusion(bf16[9,128,1024]{2,1,0:T(8,128)(2,1)S(1)} %fusion.7, s32[1024]{0:T(1024)} %pad_clamp_fusion.1), kind=kCustom, calls=%fused_computation.1 | custom fusion | bytes 8388672 | tf_op jit(solution)/shard_map/jit(_take)/gather | solution.py:95
  135.8 0.0 copy-done.2
  135.8 0.0 copy-done.3
  135.8 4.7 %select_select_fusion = bf16[16,128,1024]{2,1,0:T(8,128)(2,1)} fusion(bf16[16,128,1024]{2,1,0:T(8,128)(2,1)} %gather_fusion.1, pred[16]{0:T(512)(128)(4,1)S(1)} %copy-done.2, pred[16]{0:T(512)(128)(4,1)S(1)} %copy-done.3), kind=kLoop, calls=%fused_computation.13 | loop fusion | flops 4194304 | bytes 8388640 | tf_op jit(solution)/shard_map/jit(_where)/select_n | solution.py:93
  140.5 0.0 copy-start.5
  140.5 4.7 %all-to-all-start = ((bf16[16,128,1024]{2,1,0:T(8,128)(2,1)}), bf16[16,128,1024]{2,1,0:T(8,128)(2,1)}, u32[]{:S(2)}, u32[]{:S(2)}) async-start(bf16[16,128,1024]{2,1,0:T(8,128)(2,1)} %select_select_fusion), calls=%async_computation | async-start | bytes 8388608 | tf_op jit(solution)/shard_map/all_to_all | solution.py:98
  145.1 0.5 slice.27
  145.7 0.0 copy-done.5
  145.7 0.2 convert_reduce_fusion
  145.9 0.6 gather_fusion
  146.5 0.7 compare_and_fusion.1
  147.2 91.5 %all-to-all-done = bf16[16,128,1024]{2,1,0:T(8,128)(2,1)} async-done(((bf16[16,128,1024]{2,1,0:T(8,128)(2,1)}), bf16[16,128,1024]{2,1,0:T(8,128)(2,1)}, u32[]{:S(2)}, u32[]{:S(2)}) %all-to-all-start) | async-done | bytes 4194336 | tf_op jit(solution)/shard_map/all_to_all | solution.py:98
  238.7 2.8 %gather_fusion.2 = bf16[5,128,1024]{2,1,0:T(8,128)(2,1)S(1)} fusion(bf16[16,128,1024]{2,1,0:T(8,128)(2,1)} %all-to-all-done, s32[1024]{0:T(1024)S(1)} %pad_clamp_fusion), kind=kCustom, calls=%fused_computation.2 | custom fusion | bytes 2621460 | tf_op jit(solution)/shard_map/jit(_take)/gather | solution.py:99
  241.5 1.3 select_select_fusion.1
  (11 shorter events, 0.1 us)
Async XLA Ops:
  6.5 22.4 %copy-start.7 = (s32[1,16]{1,0:T(1,128)S(1)}, s32[1,16]{1,0:T(1,128)}, u32[]{:S(2)}) copy-start(s32[1,16]{1,0:T(1,128)} %param.6) | copy-start | bytes 196
  6.5 94.7 %all-gather.3.cloned.1.call-start = ((), (), s32[]{:S(2)}) async-start(), calls=%async_computation.1 | async-start | bytes 11141120 | tf_op jit(solution)/shard_map/all_gather | solution.py:51
  29.8 4.9 %copy-start.4 = (s32[16]{0:T(128)}, s32[16]{0:T(128)S(1)}, u32[]{:S(2)}) copy-start(s32[16]{0:T(128)S(1)} %reduce) | copy-start | bytes 196
  34.7 66.6 %copy-start.8 = (f32[5120]{0:T(1024)S(1)}, f32[5120]{0:T(1024)}, u32[]{:S(2)}) copy-start(f32[5120]{0:T(1024)} %param.8) | copy-start | bytes 61444
  122.7 2.1 copy-start.6
  124.9 1.5 copy-start
  124.9 1.5 copy-start.1
  132.9 2.9 %copy-start.2 = (pred[16]{0:T(512)(128)(4,1)S(1)}, pred[16]{0:T(512)(128)(4,1)}, u32[]{:S(2)}) copy-start(pred[16]{0:T(512)(128)(4,1)} %get-tuple-element.13) | copy-start | bytes 52
  132.9 2.9 %copy-start.3 = (pred[16]{0:T(512)(128)(4,1)S(1)}, pred[16]{0:T(512)(128)(4,1)}, u32[]{:S(2)}) copy-start(pred[16]{0:T(512)(128)(4,1)} %get-tuple-element.14) | copy-start | bytes 52
  140.5 5.2 %copy-start.5 = (s32[16]{0:T(128)S(1)}, s32[16]{0:T(128)}, u32[]{:S(2)}) copy-start(s32[16]{0:T(128)} %copy-done.4) | copy-start | bytes 196
  140.5 98.2 %all-to-all-start = ((bf16[16,128,1024]{2,1,0:T(8,128)(2,1)}), bf16[16,128,1024]{2,1,0:T(8,128)(2,1)}, u32[]{:S(2)}, u32[]{:S(2)}) async-start(bf16[16,128,1024]{2,1,0:T(8,128)(2,1)} %select_select_fusion), calls=%async_computation | async-start | bytes 8388608 | tf_op jit(solution)/shard_map/all_to_all | solution.py:98
Sparse Core Ops, SparseCore 0:
  29.1 72.1 all-gather.2
where the time goes:
time: 250 us
  waiting for transfers between devices  148 us (59%)
  other arithmetic  29.7 us (12%)
  blocking collectives  20.4 us (8%)
  matrix products  16.9 us (7%)
  local copies, waits for them, and re-layouts  16.5 us (7%)
  between operations  13.6 us (5%)
  starting transfers between devices  4.66 us (2%)
    all_to_all x1, waiting for transfers between devices, local(): lax.all_to_all(outgoing, 'tp', split_axis=0, concat_axis=0, tiled=True)  91.5 us
    all_gather x1, waiting for transfers between devices, project(): lax.all_gather(all_rows, 'tp', axis=1, tiled=True)  56.4 us
    all_gather x1, blocking collectives, project(): all_rows = lax.all_gather(kv_weight, 'grp', axis=0, tiled=True)  20.4 us
    dot_general x1, matrix products, project(): jnp.dot(normed, lax.all_gather(all_rows, 'tp', axis=1, tiled=True), prefe...  16.9 us
    reduce_sum x1, other arithmetic, normalize(): jnp.mean(values * values, axis=-1, keepdims=True) + norm_eps  6.71 us
  transfers between devices with their start and end apart: 2, of which 2 were waited for; matrix products, arithmetic and copies ran while one was open for 7% of the time, Pallas kernels for 0%

commit v1 on v0

--- a/solution.py
+++ b/solution.py
@@ -48,7 +48,9 @@
     all_rows = lax.all_gather(kv_weight, "grp", axis=0, tiled=True)
     return jnp.dot(
         normed,
-        lax.all_gather(all_rows, "tp", axis=1, tiled=True),
+        jnp.concatenate(
+            lax.all_to_all(jnp.stack([all_rows] * lax.axis_size("tp")), "tp", 0, 0), axis=1
+        ),
         preferred_element_type=jnp.float32,
     )
 

time: 250 us -> 413 us (1.65)
  waiting for transfers between devices: 148 us -> 304 us
  starting transfers between devices: 4.66 us -> 20.2 us
  between operations: 13.6 us -> 0.21 us
  local copies, waits for them, and re-layouts: 16.5 us -> 20.8 us
    all_to_all x0 -> x1, waiting for transfers between devices: none -> 212 us  [project(): lax.all_to_all(jnp.stack([all_rows] * lax.axis_size('tp')), 'tp', 0, 0)]
    all_gather x1 -> x0, waiting for transfers between devices: 56.4 us -> none  [project(): lax.all_gather(all_rows, 'tp', axis=1, tiled=True)]
    all_to_all x0 -> x1, starting transfers between devices: none -> 14.5 us  [project(): lax.all_to_all(jnp.stack([all_rows] * lax.axis_size('tp')), 'tp', 0, 0)]
    another operation x0 -> x1, local copies, waits for them, and re-layouts: none -> 5.14 us  [project(): jnp.stack([all_rows] * lax.axis_size('tp'))]
  transfers between devices with their start and end apart: 2 -> 2, of which waited for: 2 -> 2; matrix products, arithmetic and copies ran while one was open for 7% -> 4% of each run, Pallas kernels for 0% -> 0%
where the time goes in v1:
time: 413 us; the launch traced here: 412 us
  waiting for transfers between devices  304 us (74%)
  other arithmetic  29.9 us (7%)
  local copies, waits for them, and re-layouts  20.8 us (5%)
  blocking collectives  20.3 us (5%)
  starting transfers between devices  20.2 us (5%)
  matrix products  16.9 us (4%)
    all_to_all x1, waiting for transfers between devices, project(): lax.all_to_all(jnp.stack([all_rows] * lax.axis_size('tp')), 'tp', 0, 0)  212 us
    all_to_all x1, waiting for transfers between devices, local(): lax.all_to_all(outgoing, 'tp', split_axis=0, concat_axis=0, tiled=True)  91.4 us
    all_gather x1, blocking collectives, project(): all_rows = lax.all_gather(kv_weight, 'grp', axis=0, tiled=True)  20.3 us
    dot_general x1, matrix products, project(): jnp.dot(normed, jnp.concatenate(lax.all_to_all(jnp.stack([all_rows] * lax...  16.9 us
    all_to_all x1, starting transfers between devices, project(): lax.all_to_all(jnp.stack([all_rows] * lax.axis_size('tp')), 'tp', 0, 0)  14.5 us
  transfers between devices with their start and end apart: 2, of which 2 were waited for; matrix products, arithmetic and copies ran while one was open for 4% of the time, Pallas kernels for 0%

profile of v1, /device:TPU:1, one launch (start us, length us, event | category | flops | bytes accessed | tf_op | source)
XLA Modules:
  0.0 412.1 jit_solution(11193927119710140460)
XLA Ops:
  0.0 20.3 %all-gather = bf16[16,320,64]{1,2,0:T(8,128)(2,1)S(1)} all-gather(bf16[1,320,64]{1,2,0:T(8,128)(2,1)} %bitcast.47), channel_id=1, replica_groups=mesh['grp'=16,'tp'=16] {'grp'}, dimensions={0}, use_global_device_ids=true | all-gather | bytes 696320 | tf_op jit(solution)/shard_map/all_gather | solution.py:48
  20.3 0.5 copy.17
  20.7 0.6 reshape.410
  21.4 5.1 %stack.2 = bf16[16,5120,64]{1,2,0:T(8,128)(2,1)} broadcast(bf16[5120,64]{0,1:T(8,128)(2,1)S(1)} %reshape.410), dimensions={1,2} | broadcast | bytes 11141120 | tf_op jit(solution)/shard_map/stack | solution.py:52
  26.5 0.0 copy-start.7
  26.5 14.5 %all-to-all-start = ((bf16[16,5120,64]{1,2,0:T(8,128)(2,1)}), bf16[16,5120,64]{1,2,0:T(8,128)(2,1)}, u32[]{:S(2)}, u32[]{:S(2)}) async-start(bf16[16,5120,64]{1,2,0:T(8,128)(2,1)} %stack.2), calls=%async_computation | async-start | bytes 20971520 | tf_op jit(solution)/shard_map/all_to_all | solution.py:52
  41.0 0.0 copy-done.7
  41.0 0.6 constant_dynamic-slice_fusion
  41.6 0.1 copy.16
  41.7 0.1 reduce
  41.8 0.0 copy-start.4
  41.9 0.7 dynamic_slice.9
  42.5 0.6 dynamic_slice.10
  43.1 0.7 fusion.13
  43.8 1.8 compare_and_fusion
  45.6 0.6 pad_clamp_fusion.1
  46.2 0.7 fusion.8
  46.9 0.1 convert_bitcast_fusion
  47.0 0.0 copy-done.4
  47.0 0.0 copy-start.8
  47.0 6.7 %fusion = f32[1152]{0:T(1024)S(1)} fusion(bf16[1152,5120]{1,0:T(8,128)(2,1)} %param.5), kind=kLoop, calls=%fused_computation.5 | loop fusion | flops 17693568 | bytes 11801088 | tf_op jit(solution)/shard_map/reduce_sum | solution.py:16
  53.7 3.2 multiply_cosine_fusion
  57.0 212.4 %all-to-all-done = bf16[16,5120,64]{1,2,0:T(8,128)(2,1)} async-done(((bf16[16,5120,64]{1,2,0:T(8,128)(2,1)}), bf16[16,5120,64]{1,2,0:T(8,128)(2,1)}, u32[]{:S(2)}, u32[]{:S(2)}) %all-to-all-start) | async-done | bytes 10485792 | tf_op jit(solution)/shard_map/all_to_all | solution.py:52
  269.3 0.0 copy-done.8
  269.3 16.9 %fusion.3 = f32[1152,1024]{1,0:T(8,128)S(1)} fusion(bf16[5120,1024]{0,1:T(8,128)(2,1)} %bitcast.10, bf16[1152,5120]{1,0:T(8,128)(2,1)} %param.5, f32[5120]{0:T(1024)S(1)} %copy-done.8, f32[1152]{0:T(1024)S(1)} %add_rsqrt_fusion.1), kind=kOutput, calls=%fused_computation.8 | convolution fusion | flops 12103188480 | bytes 27025920 | tf_op jit(solution)/shard_map/dot_general | solution.py:49
  286.3 1.7 slice.28
  287.9 0.2 slice.31
  288.1 2.6 reshape.384
  290.8 0.0 copy-start.6
  290.8 2.0 multiply_reduce_fusion
  292.8 0.1 add_rsqrt_fusion
  292.9 0.0 copy-done.6
  292.9 0.0 copy-start
  292.9 0.0 copy-start.1
  292.9 1.5 multiply_multiply_fusion
  294.5 0.0 copy-done
  294.5 0.0 copy-done.1
  294.5 1.8 multiply_subtract_fusion
  296.3 1.9 pad_maximum_fusion
  298.2 1.3 concatenate.12
  299.5 1.7 fusion.7
  301.2 0.0 copy-start.2
  301.2 0.0 copy-start.3
  301.2 2.9 gather_fusion.1
  304.1 0.0 copy-done.2
  304.1 0.0 copy-done.3
  304.1 4.7 %select_select_fusion = bf16[16,128,1024]{2,1,0:T(8,128)(2,1)} fusion(bf16[16,128,1024]{2,1,0:T(8,128)(2,1)} %gather_fusion.1, pred[16]{0:T(512)(128)(4,1)S(1)} %copy-done.2, pred[16]{0:T(512)(128)(4,1)S(1)} %copy-done.3), kind=kLoop, calls=%fused_computation.13 | loop fusion | flops 4194304 | bytes 8388640 | tf_op jit(solution)/shard_map/jit(_where)/select_n | solution.py:95
  308.8 0.0 copy-start.5
  308.8 5.8 %all-to-all-start.1 = ((bf16[16,128,1024]{2,1,0:T(8,128)(2,1)}), bf16[16,128,1024]{2,1,0:T(8,128)(2,1)}, u32[]{:S(2)}, u32[]{:S(2)}) async-start(bf16[16,128,1024]{2,1,0:T(8,128)(2,1)} %select_select_fusion), calls=%async_computation.1 | async-start | bytes 8388608 | tf_op jit(solution)/shard_map/all_to_all | solution.py:100
  314.5 0.5 slice.27
  315.0 0.0 copy-done.5
  315.0 0.2 convert_reduce_fusion
  315.3 0.6 gather_fusion
  315.9 0.7 compare_and_fusion.1
  316.6 91.4 %all-to-all-done.1 = bf16[16,128,1024]{2,1,0:T(8,128)(2,1)} async-done(((bf16[16,128,1024]{2,1,0:T(8,128)(2,1)}), bf16[16,128,1024]{2,1,0:T(8,128)(2,1)}, u32[]{:S(2)}, u32[]{:S(2)}) %all-to-all-start.1) | async-done | bytes 4194336 | tf_op jit(solution)/shard_map/all_to_all | solution.py:100
  408.0 2.8 gather_fusion.2
  410.9 1.3 select_select_fusion.1
  (11 shorter events, 0.1 us)
Async XLA Ops:
  26.5 14.5 %copy-start.7 = (s32[1,16]{1,0:T(1,128)S(1)}, s32[1,16]{1,0:T(1,128)}, u32[]{:S(2)}) copy-start(s32[1,16]{1,0:T(1,128)} %param.6) | copy-start | bytes 196
  26.5 242.8 %all-to-all-start = ((bf16[16,5120,64]{1,2,0:T(8,128)(2,1)}), bf16[16,5120,64]{1,2,0:T(8,128)(2,1)}, u32[]{:S(2)}, u32[]{:S(2)}) async-start(bf16[16,5120,64]{1,2,0:T(8,128)(2,1)} %stack.2), calls=%async_computation | async-start | bytes 20971520 | tf_op jit(solution)/shard_map/all_to_all | solution.py:52
  41.8 5.2 %copy-start.4 = (s32[16]{0:T(128)}, s32[16]{0:T(128)S(1)}, u32[]{:S(2)}) copy-start(s32[16]{0:T(128)S(1)} %reduce) | copy-start | bytes 196
  47.0 222.3 %copy-start.8 = (f32[5120]{0:T(1024)S(1)}, f32[5120]{0:T(1024)}, u32[]{:S(2)}) copy-start(f32[5120]{0:T(1024)} %param.8) | copy-start | bytes 61444
  290.8 2.1 copy-start.6
  292.9 1.5 copy-start
  292.9 1.5 copy-start.1
  301.2 2.9 copy-start.2
  301.2 2.9 copy-start.3
  308.8 6.3 %copy-start.5 = (s32[16]{0:T(128)S(1)}, s32[16]{0:T(128)}, u32[]{:S(2)}) copy-start(s32[16]{0:T(128)} %copy-done.4) | copy-start | bytes 196
  308.8 99.3 %all-to-all-start.1 = ((bf16[16,128,1024]{2,1,0:T(8,128)(2,1)}), bf16[16,128,1024]{2,1,0:T(8,128)(2,1)}, u32[]{:S(2)}, u32[]{:S(2)}) async-start(bf16[16,128,1024]{2,1,0:T(8,128)(2,1)} %select_select_fusion), calls=%async_computation.1 | async-start | bytes 8388608 | tf_op jit(solution)/shard_map/all_to_all | solution.py:100
